TPU v7x, 32 devices: a whole 2x2x4 slice. The times are simulated.
32 devices in a mesh: param: 4 (over y, x), ex: 8 (over z, core).
Axes of the slice: x: 2, y: 2, z: 4, core: 2. Of those that a mesh axis runs over, the one named last changes fastest.
Arguments:
- activations: bfloat16 [64, 32, 4096], P('ex', None, 'param'), may hold values from -24 to 24
- output_gradients: bfloat16 [2, 64, 32, 4096], P(None, 'ex', None, 'param'), may hold values from -24 to 24
- down_projection_weight: bfloat16 [2, 16, 4096], P(None, None, 'param'), may hold values from -0.09375 to 0.09375
- adapter_up: bfloat16 [2, 4096, 16], P(None, 'param'), may hold values from -0.09375 to 0.09375
- projection: bfloat16 [262144, 4096], P(('param', 'ex')), may hold values from -0.111328125 to 0.111328125
- domains: int32 [64], P('ex'), may hold values from 0 to 3
- target_ids: int32 [256], P('param'), may hold values from 0 to 63
Outputs:
- scores: float32 [256, 64], P('param', 'ex')
- domain_scores: float32 [256, 4], P('param')
All inputs are finite; a program needn't handle non-finite values.
Results may differ from a plain program's by a relative error of at most 0.0059.
Values may be sent and summed in bfloat16 or wider, within the bound.
No kernel may reach another device: no remote copies, remote signals or barrier semaphores. Data moves between devices by JAX's collectives and lax.ppermute only.
A program may use at most 192 MiB of HBM per device.

v0:
```python
import math
import jax
import jax.numpy as jnp
from jax import lax
from jax.sharding import PartitionSpec as P

K = 4096
DOMAINS = 4


def inner_rows(left, right):
    return lax.dot_general(
        left,
        right,
        (((0,), (0,)), ((), ())),
        precision=lax.Precision.HIGHEST,
        preferred_element_type=jnp.float32,
    )


def local(
    activations,
    output_gradients,
    down_projection_weight,
    adapter_up,
    projection,
    domains,
    target_ids,
):
    single_float = jnp.float32
    ex_rows = activations.shape[0]
    adapter_rank_size = down_projection_weight.shape[1]
    up_terms = jnp.einsum(
        "ansd,adr->ansr", output_gradients, adapter_up, preferred_element_type=single_float
    )
    down_terms = jnp.einsum(
        "nsd,ard->ansr", activations, down_projection_weight, preferred_element_type=single_float
    )
    partial_low = jnp.concatenate([up_terms[0], up_terms[1], down_terms[0], down_terms[1]], axis=-1)
    rank_factor = lax.psum(partial_low, "param").astype(jnp.bfloat16)
    first = jnp.einsum(
        "erb,ery->eby",
        activations,
        rank_factor[..., : 2 * adapter_rank_size],
        preferred_element_type=single_float,
    )
    second = jnp.einsum(
        "fai,fav->fiv",
        output_gradients[0],
        rank_factor[..., 2 * adapter_rank_size : 3 * adapter_rank_size],
        preferred_element_type=single_float,
    )
    third = jnp.einsum(
        "fai,fav->fiv",
        output_gradients[1],
        rank_factor[..., 3 * adapter_rank_size :],
        preferred_element_type=single_float,
    )
    grads = jnp.concatenate([first, second, third], axis=-1).astype(jnp.bfloat16)
    grads = grads.reshape(ex_rows, grads.shape[1] * grads.shape[2])
    column_indices = lax.all_to_all(grads, "ex", split_axis=1, concat_axis=0, tiled=True)
    features = lax.psum_scatter(
        lax.dot_general(
            projection,
            column_indices,
            (((0,), (1,)), ((), ())),
            preferred_element_type=single_float,
        ),
        ("param", "ex"),
        scatter_dimension=0,
        tiled=True,
    )
    totals = lax.psum(jnp.sum(features * features, axis=0), ("param", "ex"))
    unit_rows = features * lax.rsqrt(totals + 1e-06)[None, :]
    gram = lax.psum(inner_rows(unit_rows, unit_rows), ("param", "ex"))
    example_count = gram.shape[0]
    kernel = gram + 0.25 * jnp.eye(example_count, dtype=single_float)
    lower = jnp.linalg.cholesky(kernel)
    first_row = lax.axis_index("ex") * ex_rows
    picks = (
        jnp.arange(example_count, dtype=jnp.int32)[:, None]
        == first_row + jnp.arange(ex_rows, dtype=jnp.int32)[None, :]
    ).astype(single_float)
    inverse_cols = jax.scipy.linalg.cho_solve((lower, True), picks)
    cross = jnp.take(gram, target_ids, axis=0)
    selfmask = target_ids[:, None] == jnp.arange(example_count, dtype=jnp.int32)[None, :]
    cross = jnp.where(selfmask, jnp.zeros_like(cross), cross)
    scores = math.sqrt(K) * jnp.dot(
        cross, inverse_cols, precision=lax.Precision.HIGHEST, preferred_element_type=single_float
    )
    indicator_matrix = (domains[:, None] == jnp.arange(DOMAINS, dtype=jnp.int32)[None, :]).astype(
        single_float
    )
    domain_partial_sums = jnp.dot(
        scores,
        indicator_matrix,
        precision=lax.Precision.HIGHEST,
        preferred_element_type=single_float,
    )
    domain_scores = lax.psum(domain_partial_sums, "ex") / math.sqrt(example_count / DOMAINS)
    return (scores, domain_scores)


def solution(mesh):
    in_specs = (
        P("ex", None, "param"),
        P(None, "ex", None, "param"),
        P(None, None, "param"),
        P(None, "param", None),
        P(("param", "ex"), None),
        P("ex"),
        P("param"),
    )
    out_specs = (P("param", "ex"), P("param", None))
    return jax.shard_map(local, mesh=mesh, in_specs=in_specs, out_specs=out_specs, check_vma=False)
```

profile of v0, /device:TPU:0, one launch (start us, length us, event | category | flops | bytes accessed | tf_op | source)
XLA Modules:
  0.0 345.9 jit_solution(10288716785213548179)
XLA Ops:
  7.2 0.0 reduce-scatter.2.cloned.1.call-start
  7.2 1.0 copy-done
  8.2 1.3 convolution_bitcast_fusion.1
  9.6 2.0 fusion.11
  11.7 22.6 %psum.28 = bf16[8,32,64]{1,2,0:T(8,128)(2,1)S(1)} all-reduce(f32[8,32,64]{1,2,0:T(8,128)S(1)} %pad_maximum_fusion.1), channel_id=1, replica_groups=mesh['param'=4,'ex'=8] {'param'}, use_global_device_ids=true, to_apply=%region_0.0 | all-reduce | flops 16384 | bytes 98304 | tf_op jit(solution)/shard_map/psum | solution.py:40
  34.3 0.3 fusion
  34.6 0.2 fusion.1
  34.8 0.2 fusion.2
  35.0 1.1 pad_maximum_fusion
  36.1 2.0 copy.13
  38.2 2.5 convert_element_type.13
  40.7 1.8 copy.14
  42.5 31.3 %all_to_all.16 = bf16[8,8,8192]{2,0,1:T(8,128)(2,1)S(1)} all-to-all(bf16[8,8,8192]{2,0,1:T(8,128)(2,1)S(1)} %copy.14), channel_id=1, replica_groups=mesh['param'=4,'ex'=8] {'ex'}, dimensions={1} | all-to-all | bytes 2097152 | tf_op jit(solution)/shard_map/all_to_all | solution.py:61
  73.7 24.4 %convolution_bitcast_fusion = f32[4096,64]{0,1:T(8,128)} fusion(bf16[8192,4096]{1,0:T(8,128)(2,1)} %param.11, bf16[8,8,8192]{2,0,1:T(8,128)(2,1)S(1)} %all_to_all.16), kind=kOutput, calls=%fused_computation.1 | convolution fusion | flops 4294967296 | bytes 69206016 | tf_op jit(solution)/shard_map/dot_general | solution.py:63
  98.1 0.0 reduce-scatter.2.cloned.1.call-update
  98.2 132.3 %reduce-scatter.2.cloned.1.call-done = f32[128,64]{0,1:T(8,128)} async-done(((f32[4096,64]{0,1:T(8,128)}), f32[128,64]{0,1:T(8,128)}) %reduce-scatter.2.cloned.1.call-update) | async-done | bytes 32784 | tf_op jit(solution)/shard_map/reduce_scatter | solution.py:62
  230.5 0.9 multiply_reduce_fusion
  231.3 36.9 %psum.29 = f32[64]{0:T(128)S(1)} all-reduce(f32[64]{0:T(128)S(1)} %multiply_reduce_fusion), channel_id=1, replica_groups=mesh['param'=4,'ex'=8] {'param','ex'}, use_global_device_ids=true, to_apply=%region_3.0 | all-reduce | flops 64 | bytes 512 | tf_op jit(solution)/shard_map/psum | solution.py:73
  268.2 1.1 fusion.23
  269.3 41.6 %psum.30 = f32[64,64]{1,0:T(8,128)S(1)} all-reduce(f32[64,64]{1,0:T(8,128)S(1)} %fusion.23), channel_id=1, replica_groups=mesh['param'=4,'ex'=8] {'param','ex'}, use_global_device_ids=true, to_apply=%region_4.0 | all-reduce | flops 4096 | bytes 32768 | tf_op jit(solution)/shard_map/psum | solution.py:75
  310.9 0.1 copy.15
  311.0 5.8 %cholesky.15 = f32[64,64]{1,0:T(8,128)S(1)} custom-call(f32[64,64]{1,0:T(8,128)S(1)} %fusion.20), custom_call_target="Cholesky" | custom-call | tf_op jit(solution)/shard_map/jit(cholesky)/cholesky | solution.py:78
  316.9 0.6 compare_reduce_fusion
  317.5 0.7 fusion.13
  318.2 4.9 %custom-call.10 = f32[1,64,64]{1,2,0:T(8,128)S(1)} custom-call(f32[1,64,64]{2,1,0:T(8,128)S(1)} %fusion.13), custom_call_target="InvertDiagBlocksLowerTriangular" | custom-call | tf_op jit(solution)/shard_map/jit(_cho_solve)/triangular_solve | solution.py:84
  323.1 0.2 fusion.18
  323.3 0.2 fusion.16
  323.5 0.6 gather_fusion
  324.1 0.2 convolution_multiply_fusion
  324.3 0.3 fusion.31
  324.6 13.9 %psum.31 = f32[64,4]{0,1:T(4,128)S(1)} all-reduce(f32[64,4]{0,1:T(4,128)S(1)} %fusion.31), channel_id=1, replica_groups=mesh['param'=4,'ex'=8] {'ex'}, use_global_device_ids=true, to_apply=%region_7.8 | all-reduce | flops 256 | bytes 2048 | tf_op jit(solution)/shard_map/psum | solution.py:100
  338.4 0.6 broadcast_multiply_fusion
  (19 shorter events, 0.2 us)
Async XLA Ops:
  7.2 1.0 copy-start
  7.2 27.4 %copy-start.1 = (bf16[2,8,32,1024]{3,2,1,0:T(8,128)(2,1)S(1)}, bf16[2,8,32,1024]{3,2,1,0:T(8,128)(2,1)}, u32[]{:S(2)}) copy-start(bf16[2,8,32,1024]{3,2,1,0:T(8,128)(2,1)} %param.8) | copy-start | bytes 3145732
  7.2 223.3 %reduce-scatter.2.cloned.1.call-start = ((), (), s32[]{:S(2)}) async-start(), calls=%async_computation.2 | async-start | bytes 1081344 | tf_op jit(solution)/shard_map/reduce_scatter | solution.py:62
  73.7 24.4 %copy-start.2 = (s32[64]{0:T(128)S(1)}, s32[64]{0:T(128)}, u32[]{:S(2)}) copy-start(s32[64]{0:T(128)} %param.13) | copy-start | bytes 772
  73.7 250.6 %copy-start.3 = (s32[8]{0:T(128)S(1)}, s32[8]{0:T(128)}, u32[]{:S(2)}) copy-start(s32[8]{0:T(128)} %param.12) | copy-start | bytes 100
  324.3 14.7 %copy-start.4 = (f32[64,8]{0,1:T(8,128)}, f32[64,8]{0,1:T(8,128)S(1)}, u32[]{:S(2)}) copy-start(f32[64,8]{0,1:T(8,128)S(1)} %convolution_multiply_fusion) | copy-start | bytes 6148
Sparse Core Ops, SparseCore 0:
  98.3 132.1 reduce-scatter.1
where the time goes:
time: 346 us
  blocking collectives  146 us (42%)
  waiting for transfers between devices  132 us (38%)
  matrix products  30.4 us (9%)
  other arithmetic  14.7 us (4%)
  between operations  14.2 us (4%)
  local copies, waits for them, and re-layouts  8.06 us (2%)
    reduce_scatter x1, waiting for transfers between devices, local(): lax.psum_scatter(lax.dot_general(projection, column_indices, (((0,), (1,)...  132 us
    psum x1, blocking collectives, local(): gram = lax.psum(inner_rows(unit_rows, unit_rows), ('param', 'ex'))  41.6 us
    psum x1, blocking collectives, local(): totals = lax.psum(jnp.sum(features * features, axis=0), ('param', 'ex'))  36.9 us
    all_to_all x1, blocking collectives, local(): lax.all_to_all(grads, 'ex', split_axis=1, concat_axis=0, tiled=True)  31.3 us
    dot_general x1, matrix products, local(): lax.dot_general(projection, column_indices, (((0,), (1,)), ((), ())), pre...  24.4 us
    psum x1, blocking collectives, local(): rank_factor = lax.psum(partial_low, 'param').astype(jnp.bfloat16)  22.6 us
    psum x1, blocking collectives, local(): lax.psum(domain_partial_sums, 'ex') / math.sqrt(example_count / DOMAINS)  13.9 us
  transfers between devices with their start and end apart: 1, of which 1 were waited for; matrix products, arithmetic and copies ran while one was open for 0% of the time, Pallas kernels for 0%

commit v1 on v0

--- a/solution.py
+++ b/solution.py
@@ -6,6 +6,17 @@
 
 K = 4096
 DOMAINS = 4
+
+
+def cut_along(x, dim, size):
+    before, after = (x.shape[:dim], x.shape[dim + 1 :])
+    return jnp.moveaxis(x.reshape(*before, size, -1, *after), dim, 0)
+
+
+def laid_out(tiles, dim):
+    lengths = list(tiles.shape[1:])
+    lengths[dim] *= tiles.shape[0]
+    return jnp.moveaxis(tiles, 0, dim).reshape(lengths)
 
 
 def inner_rows(left, right):
@@ -58,7 +69,15 @@
     )
     grads = jnp.concatenate([first, second, third], axis=-1).astype(jnp.bfloat16)
     grads = grads.reshape(ex_rows, grads.shape[1] * grads.shape[2])
-    column_indices = lax.all_to_all(grads, "ex", split_axis=1, concat_axis=0, tiled=True)
+    length, mine = (lax.axis_size("ex"), lax.axis_index("ex"))
+    tiles = cut_along(grads, 1, length)
+    out = tiles
+    for step in range(1, length):
+        target, source = ((mine + step) % length, (mine - step) % length)
+        sent = lax.dynamic_index_in_dim(tiles, target, 0)
+        other = lax.ppermute(sent, "ex", [(i, (i + step) % length) for i in range(length)])
+        out = lax.dynamic_update_slice_in_dim(out, other, source, axis=0)
+    column_indices = laid_out(out, 0)
     features = lax.psum_scatter(
         lax.dot_general(
             projection,

time: 346 us -> 381 us (1.10)
  blocking collectives: 146 us -> 115 us
  local copies, waits for them, and re-layouts: 8.06 us -> 37.1 us
  waiting for transfers between devices: 132 us -> 156 us
  starting transfers between devices: 0.04 us -> 13.2 us
    all_to_all x1 -> x0, blocking collectives: 31.3 us -> none  [local(): lax.all_to_all(grads, 'ex', split_axis=1, concat_axis=0, tiled=True)]
    dynamic_update_slice x0 -> x7, local copies, waits for them, and re-layouts: none -> 27.5 us  [local(): out = lax.dynamic_update_slice_in_dim(out, other, source, axis=0)]
    ppermute x0 -> x7, starting transfers between devices: none -> 13.2 us  [local(): lax.ppermute(sent, 'ex', [(i, (i + step) % length) for i in range(length)])]
    reduce_scatter x1, waiting for transfers between devices: 132 us -> 145 us  [local(): lax.psum_scatter(lax.dot_general(projection, column_indices, (((0,), (1,)...]
    ppermute x0 -> x7, waiting for transfers between devices: none -> 11.8 us  [local(): lax.ppermute(sent, 'ex', [(i, (i + step) % length) for i in range(length)])]
  transfers between devices with their start and end apart: 1 -> 8, of which waited for: 1 -> 3; matrix products, arithmetic and copies ran while one was open for 0% -> 6% of each run, Pallas kernels for 0% -> 0%
where the time goes in v1:
time: 381 us; the launch traced here: 380 us
  waiting for transfers between devices  156 us (41%)
  blocking collectives  115 us (30%)
  local copies, waits for them, and re-layouts  37.1 us (10%)
  matrix products  30.4 us (8%)
  between operations  14.5 us (4%)
  other arithmetic  13.7 us (4%)
  starting transfers between devices  13.2 us (3%)
    reduce_scatter x1, waiting for transfers between devices, local(): lax.psum_scatter(lax.dot_general(projection, column_indices, (((0,), (1,)...  145 us
    psum x1, blocking collectives, local(): gram = lax.psum(inner_rows(unit_rows, unit_rows), ('param', 'ex'))  41.8 us
    psum x1, blocking collectives, local(): totals = lax.psum(jnp.sum(features * features, axis=0), ('param', 'ex'))  36.9 us
    dynamic_update_slice x7, local copies, waits for them, and re-layouts, local(): out = lax.dynamic_update_slice_in_dim(out, other, source, axis=0)  27.5 us
    dot_general x1, matrix products, local(): lax.dot_general(projection, column_indices, (((0,), (1,)), ((), ())), pre...  24.3 us
    psum x1, blocking collectives, local(): rank_factor = lax.psum(partial_low, 'param').astype(jnp.bfloat16)  22.6 us
    psum x1, blocking collectives, local(): lax.psum(domain_partial_sums, 'ex') / math.sqrt(example_count / DOMAINS)  13.8 us
    ppermute x7, starting transfers between devices, local(): lax.ppermute(sent, 'ex', [(i, (i + step) % length) for i in range(length)])  13.2 us
  transfers between devices with their start and end apart: 8, of which 3 were waited for; matrix products, arithmetic and copies ran while one was open for 6% of the time, Pallas kernels for 0%

profile of v1, /device:TPU:0, one launch (start us, length us, event | category | flops | bytes accessed | tf_op | source)
XLA Modules:
  0.0 380.4 jit_solution(6355711898327513600)
XLA Ops:
  7.3 0.9 copy-done
  8.2 1.4 convolution_bitcast_fusion.1
  9.6 2.0 fusion.12
  11.7 22.6 %psum.28 = bf16[8,32,64]{1,2,0:T(8,128)(2,1)S(1)} all-reduce(f32[8,32,64]{1,2,0:T(8,128)S(1)} %pad_maximum_fusion.1), channel_id=1, replica_groups=mesh['param'=4,'ex'=8] {'param'}, use_global_device_ids=true, to_apply=%region_0.0 | all-reduce | flops 16384 | bytes 98304 | tf_op jit(solution)/shard_map/psum | solution.py:51
  35.2 1.8 copy.10
  37.0 3.3 convert_element_type.12
  40.4 2.9 dynamic-slice_bitcast_fusion
  43.2 1.6 collective-permute-start.1
  44.8 2.6 collective-permute-start.2
  47.4 1.2 collective-permute-start.3
  48.6 1.2 collective-permute-start.4
  49.8 3.5 collective-permute-done
  53.3 1.6 collective-permute-start.5
  54.9 5.0 %collective-permute-start.6 = (bf16[1,8,8192]{2,0,1:T(2,128)(2,1)}, bf16[1,8,8192]{2,0,1:T(2,128)(2,1)S(1)}, u32[]{:S(2)}, u32[]{:S(2)}) collective-permute-start(bf16[1,8,8192]{2,0,1:T(2,128)(2,1)} %get-tuple-element.2), channel_id=1, source_target_pairs={{0,7},{1,0},{2,1},{3,2},{4,3},{5,4},{6,5},{7,6},{8,15},{9,8},{10,9... | collective-permute-start | bytes 393224 | tf_op jit(solution)/shard_map/ppermute | solution.py:78
  59.9 3.9 %dynamic_update_slice.21 = bf16[8,8,8192]{2,0,1:T(8,128)(2,1)S(1)} dynamic-update-slice(bf16[8,8,8192]{2,0,1:T(8,128)(2,1)S(1)} %bitcast.72, bf16[1,8,8192]{2,0,1:T(2,128)(2,1)S(1)} %collective-permute-done, s32[]{:T(128)S(6)} %select_n.123, s32[]{:T(128)} %constant.162.clone.1, s32[]{:T(128)} %constant.162.clone.1) | dynamic-update-slice | bytes 262148 | tf_op jit(solution)/shard_map/dynamic_update_slice | solution.py:79
  63.8 3.9 %dynamic_update_slice.22 = bf16[8,8,8192]{2,0,1:T(8,128)(2,1)S(1)} dynamic-update-slice(bf16[8,8,8192]{2,0,1:T(8,128)(2,1)S(1)} %dynamic_update_slice.21, bf16[1,8,8192]{2,0,1:T(2,128)(2,1)S(1)} %collective-permute-done.1, s32[]{:T(128)S(6)} %select_n.127, s32[]{:T(128)} %constant.162.clone.1, s32[]{:T(128)} %constant.162.clone.1) | dynamic-update-slice | bytes 262148 | tf_op jit(solution)/shard_map/dynamic_update_slice | solution.py:79
  67.8 8.3 %collective-permute-done.2 = bf16[1,8,8192]{2,0,1:T(2,128)(2,1)S(1)} collective-permute-done((bf16[1,8,8192]{2,0,1:T(2,128)(2,1)}, bf16[1,8,8192]{2,0,1:T(2,128)(2,1)S(1)}, u32[]{:S(2)}, u32[]{:S(2)}) %collective-permute-start.2) | collective-permute-done | bytes 131104 | tf_op jit(solution)/shard_map/ppermute | solution.py:78
  76.1 3.9 %dynamic_update_slice.23 = bf16[8,8,8192]{2,0,1:T(8,128)(2,1)S(1)} dynamic-update-slice(bf16[8,8,8192]{2,0,1:T(8,128)(2,1)S(1)} %dynamic_update_slice.22, bf16[1,8,8192]{2,0,1:T(2,128)(2,1)S(1)} %collective-permute-done.2, s32[]{:T(128)S(6)} %select_n.131, s32[]{:T(128)} %constant.162.clone.1, s32[]{:T(128)} %constant.162.clone.1) | dynamic-update-slice | bytes 262148 | tf_op jit(solution)/shard_map/dynamic_update_slice | solution.py:79
  80.0 3.9 %dynamic_update_slice.24 = bf16[8,8,8192]{2,0,1:T(8,128)(2,1)S(1)} dynamic-update-slice(bf16[8,8,8192]{2,0,1:T(8,128)(2,1)S(1)} %dynamic_update_slice.23, bf16[1,8,8192]{2,0,1:T(2,128)(2,1)S(1)} %collective-permute-done.3, s32[]{:T(128)S(6)} %select_n.135, s32[]{:T(128)} %constant.162.clone.1, s32[]{:T(128)} %constant.162.clone.1) | dynamic-update-slice | bytes 262148 | tf_op jit(solution)/shard_map/dynamic_update_slice | solution.py:79
  83.9 3.9 %dynamic_update_slice.25 = bf16[8,8,8192]{2,0,1:T(8,128)(2,1)S(1)} dynamic-update-slice(bf16[8,8,8192]{2,0,1:T(8,128)(2,1)S(1)} %dynamic_update_slice.24, bf16[1,8,8192]{2,0,1:T(2,128)(2,1)S(1)} %collective-permute-done.4, s32[]{:T(128)S(6)} %select_n.139, s32[]{:T(128)} %constant.162.clone.1, s32[]{:T(128)} %constant.162.clone.1) | dynamic-update-slice | bytes 262148 | tf_op jit(solution)/shard_map/dynamic_update_slice | solution.py:79
  87.9 3.9 %dynamic_update_slice.26 = bf16[8,8,8192]{2,0,1:T(8,128)(2,1)S(1)} dynamic-update-slice(bf16[8,8,8192]{2,0,1:T(8,128)(2,1)S(1)} %dynamic_update_slice.25, bf16[1,8,8192]{2,0,1:T(2,128)(2,1)S(1)} %collective-permute-done.5, s32[]{:T(128)S(6)} %select_n.143, s32[]{:T(128)} %constant.162.clone.1, s32[]{:T(128)} %constant.162.clone.1) | dynamic-update-slice | bytes 262148 | tf_op jit(solution)/shard_map/dynamic_update_slice | solution.py:79
  91.8 3.9 %dynamic_update_slice.27 = bf16[8,8,8192]{2,0,1:T(8,128)(2,1)S(1)} dynamic-update-slice(bf16[8,8,8192]{2,0,1:T(8,128)(2,1)S(1)} %dynamic_update_slice.26, bf16[1,8,8192]{2,0,1:T(2,128)(2,1)S(1)} %collective-permute-done.6, s32[]{:T(128)S(6)} %select_n.147, s32[]{:T(128)} %constant.162.clone.1, s32[]{:T(128)} %constant.162.clone.1) | dynamic-update-slice | bytes 262148 | tf_op jit(solution)/shard_map/dynamic_update_slice | solution.py:79
  95.8 24.3 %convolution_bitcast_fusion = f32[4096,64]{0,1:T(8,128)} fusion(bf16[8192,4096]{1,0:T(8,128)(2,1)} %param.11, bf16[8,8,8192]{2,0,1:T(8,128)(2,1)S(1)} %dynamic_update_slice.27), kind=kOutput, calls=%fused_computation.1 | convolution fusion | flops 4294967296 | bytes 69206016 | tf_op jit(solution)/shard_map/dot_general | solution.py:82
  120.2 144.6 %reduce-scatter.2.cloned.1.call-done = f32[128,64]{0,1:T(8,128)} async-done(((f32[4096,64]{0,1:T(8,128)}), f32[128,64]{0,1:T(8,128)}) %reduce-scatter.2.cloned.1.call-update) | async-done | bytes 32784 | tf_op jit(solution)/shard_map/reduce_scatter | solution.py:81
  264.8 0.9 multiply_reduce_fusion
  265.7 36.9 %psum.29 = f32[64]{0:T(128)S(1)} all-reduce(f32[64]{0:T(128)S(1)} %multiply_reduce_fusion), channel_id=1, replica_groups=mesh['param'=4,'ex'=8] {'param','ex'}, use_global_device_ids=true, to_apply=%region_3.4 | all-reduce | flops 64 | bytes 512 | tf_op jit(solution)/shard_map/psum | solution.py:92
  302.6 1.1 fusion.24
  303.6 41.8 %psum.30 = f32[64,64]{1,0:T(8,128)S(1)} all-reduce(f32[64,64]{1,0:T(8,128)S(1)} %fusion.24), channel_id=1, replica_groups=mesh['param'=4,'ex'=8] {'param','ex'}, use_global_device_ids=true, to_apply=%region_4.5 | all-reduce | flops 4096 | bytes 32768 | tf_op jit(solution)/shard_map/psum | solution.py:94
  345.6 5.8 %cholesky.15 = f32[64,64]{1,0:T(8,128)S(1)} custom-call(f32[64,64]{1,0:T(8,128)S(1)} %fusion.21), custom_call_target="Cholesky" | custom-call | tf_op jit(solution)/shard_map/jit(cholesky)/cholesky | solution.py:97
  352.1 0.7 fusion.14
  352.7 4.9 %custom-call.10 = f32[1,64,64]{1,2,0:T(8,128)S(1)} custom-call(f32[1,64,64]{2,1,0:T(8,128)S(1)} %fusion.14), custom_call_target="InvertDiagBlocksLowerTriangular" | custom-call | tf_op jit(solution)/shard_map/jit(_cho_solve)/triangular_solve | solution.py:103
  359.1 13.8 %psum.31 = f32[64,4]{0,1:T(4,128)S(1)} all-reduce(f32[64,4]{0,1:T(4,128)S(1)} %fusion.32), channel_id=1, replica_groups=mesh['param'=4,'ex'=8] {'ex'}, use_global_device_ids=true, to_apply=%region_7.8 | all-reduce | flops 256 | bytes 2048 | tf_op jit(solution)/shard_map/psum | solution.py:119
  (39 shorter events, 3.8 us)
Async XLA Ops:
  7.2 1.0 copy-start
  7.2 257.6 %reduce-scatter.2.cloned.1.call-start = ((), (), s32[]{:S(2)}) async-start(), calls=%async_computation.1 | async-start | bytes 1081344 | tf_op jit(solution)/shard_map/reduce_scatter | solution.py:81
  8.2 26.5 %copy-start.1 = (bf16[2,8,32,1024]{3,2,1,0:T(8,128)(2,1)S(1)}, bf16[2,8,32,1024]{3,2,1,0:T(8,128)(2,1)}, u32[]{:S(2)}) copy-start(bf16[2,8,32,1024]{3,2,1,0:T(8,128)(2,1)} %param.8) | copy-start | bytes 3145732
  43.2 10.0 %collective-permute-start = (bf16[1,8,8192]{2,0,1:T(2,128)(2,1)S(1)}, bf16[1,8,8192]{2,0,1:T(2,128)(2,1)S(1)}, u32[]{:S(2)}, u32[]{:S(2)}) collective-permute-start(bf16[1,8,8192]{2,0,1:T(2,128)(2,1)S(1)} %get-tuple-element.8), channel_id=1, source_target_pairs={{0,1},{1,2},{2,3},{3,4},{4,5},{5,6},{6,7},{7,0},{8,9},{9,10},{10,1... | collective-permute-start | bytes 393224 | tf_op jit(solution)/shard_map/ppermute | solution.py:78
  43.2 11.7 %collective-permute-start.1 = (bf16[1,8,8192]{2,0,1:T(2,128)(2,1)S(1)}, bf16[1,8,8192]{2,0,1:T(2,128)(2,1)S(1)}, u32[]{:S(2)}, u32[]{:S(2)}) collective-permute-start(bf16[1,8,8192]{2,0,1:T(2,128)(2,1)S(1)} %get-tuple-element.7), channel_id=1, source_target_pairs={{0,2},{1,3},{2,4},{3,5},{4,6},{5,7},{6,0},{7,1},{8,10},{9,11},{10,... | collective-permute-start | bytes 393224 | tf_op jit(solution)/shard_map/ppermute | solution.py:78
  44.8 31.2 %collective-permute-start.2 = (bf16[1,8,8192]{2,0,1:T(2,128)(2,1)}, bf16[1,8,8192]{2,0,1:T(2,128)(2,1)S(1)}, u32[]{:S(2)}, u32[]{:S(2)}) collective-permute-start(bf16[1,8,8192]{2,0,1:T(2,128)(2,1)} %get-tuple-element.6), channel_id=1, source_target_pairs={{0,3},{1,4},{2,5},{3,6},{4,7},{5,0},{6,1},{7,2},{8,11},{9,12},{10,... | collective-permute-start | bytes 393224 | tf_op jit(solution)/shard_map/ppermute | solution.py:78
  47.4 32.6 %collective-permute-start.3 = (bf16[1,8,8192]{2,0,1:T(2,128)(2,1)}, bf16[1,8,8192]{2,0,1:T(2,128)(2,1)S(1)}, u32[]{:S(2)}, u32[]{:S(2)}) collective-permute-start(bf16[1,8,8192]{2,0,1:T(2,128)(2,1)} %get-tuple-element.5), channel_id=1, source_target_pairs={{0,4},{1,5},{2,6},{3,7},{4,0},{5,1},{6,2},{7,3},{8,12},{9,13},{10,... | collective-permute-start | bytes 393224 | tf_op jit(solution)/shard_map/ppermute | solution.py:78
  48.6 35.3 %collective-permute-start.4 = (bf16[1,8,8192]{2,0,1:T(2,128)(2,1)}, bf16[1,8,8192]{2,0,1:T(2,128)(2,1)S(1)}, u32[]{:S(2)}, u32[]{:S(2)}) collective-permute-start(bf16[1,8,8192]{2,0,1:T(2,128)(2,1)} %get-tuple-element.4), channel_id=1, source_target_pairs={{0,5},{1,6},{2,7},{3,0},{4,1},{5,2},{6,3},{7,4},{8,13},{9,14},{10,... | collective-permute-start | bytes 393224 | tf_op jit(solution)/shard_map/ppermute | solution.py:78
  53.3 34.6 %collective-permute-start.5 = (bf16[1,8,8192]{2,0,1:T(2,128)(2,1)}, bf16[1,8,8192]{2,0,1:T(2,128)(2,1)S(1)}, u32[]{:S(2)}, u32[]{:S(2)}) collective-permute-start(bf16[1,8,8192]{2,0,1:T(2,128)(2,1)} %get-tuple-element.3), channel_id=1, source_target_pairs={{0,6},{1,7},{2,0},{3,1},{4,2},{5,3},{6,4},{7,5},{8,14},{9,15},{10,... | collective-permute-start | bytes 393224 | tf_op jit(solution)/shard_map/ppermute | solution.py:78
  54.9 36.9 %collective-permute-start.6 = (bf16[1,8,8192]{2,0,1:T(2,128)(2,1)}, bf16[1,8,8192]{2,0,1:T(2,128)(2,1)S(1)}, u32[]{:S(2)}, u32[]{:S(2)}) collective-permute-start(bf16[1,8,8192]{2,0,1:T(2,128)(2,1)} %get-tuple-element.2), channel_id=1, source_target_pairs={{0,7},{1,0},{2,1},{3,2},{4,3},{5,4},{6,5},{7,6},{8,15},{9,8},{10,9... | collective-permute-start | bytes 393224 | tf_op jit(solution)/shard_map/ppermute | solution.py:78
  95.8 24.4 %copy-start.2 = (s32[64]{0:T(128)S(1)}, s32[64]{0:T(128)}, u32[]{:S(2)}) copy-start(s32[64]{0:T(128)} %param.13) | copy-start | bytes 772
  120.1 238.8 %copy-start.3 = (s32[8]{0:T(128)S(1)}, s32[8]{0:T(128)}, u32[]{:S(2)}) copy-start(s32[8]{0:T(128)} %param.12) | copy-start | bytes 100
  358.9 14.7 %copy-start.4 = (f32[64,8]{0,1:T(8,128)}, f32[64,8]{0,1:T(8,128)S(1)}, u32[]{:S(2)}) copy-start(f32[64,8]{0,1:T(8,128)S(1)} %convolution_multiply_fusion) | copy-start | bytes 6148
Sparse Core Ops, SparseCore 0:
  120.3 144.4 reduce-scatter.1
